TPU v7x, 32 devices: a whole 2x2x4 slice. The times are simulated.
32 devices in a mesh: dp: 4 (over y, x), tile: 8 (over z, core).
Axes of the slice: x: 2, y: 2, z: 4, core: 2. Of those that a mesh axis runs over, the one named last changes fastest.
Arguments:
- features: bfloat16 [4, 8, 512, 1280], P('dp', 'tile'), may hold values from -6 to 6
- visible: int32 [4, 8, 512], P('dp', 'tile'), may hold values from 0 to 1, as said below
- positions: int32 [4, 8, 512], P('dp', 'tile'), may hold values from 0 to 511, each once within a row
- cotangent: bfloat16 [4, 8, 512, 512], P('dp', 'tile'), may hold values from -6 to 6
- mlp_gain: float32 [1280], replicated, may hold values from 0.1 to 1.9
- mlp_bias: float32 [1280], replicated, may hold values from -3 to 3
- fc1_weight: bfloat16 [1280, 2560], replicated, may hold values from -0.15625 to 0.15625
- fc1_bias: float32 [2560], replicated, may hold values from -3 to 3
- fc2_weight: bfloat16 [2560, 1280], replicated, may hold values from -0.125 to 0.125
- fc2_bias: float32 [1280], replicated, may hold values from -3 to 3
- encoder_gain: float32 [1280], replicated, may hold values from 0.1 to 1.9
- encoder_bias: float32 [1280], replicated, may hold values from -3 to 3
- embed_weight: bfloat16 [1280, 512], replicated, may hold values from -0.15625 to 0.15625
- embed_bias: float32 [512], replicated, may hold values from -3 to 3
- mask_token: float32 [512], replicated, may hold values from -4 to 4
- position_table: bfloat16 [512, 512], replicated, may hold values from -4 to 4
- decoder_gain: float32 [512], replicated, may hold values from 0.1 to 1.9
- decoder_bias: float32 [512], replicated, may hold values from -3 to 3
Outputs:
- feature_grad: bfloat16 [4, 8, 512, 1280], P('dp', 'tile')
- decoded: bfloat16 [4, 8, 512, 512], P('dp', 'tile')
- fc1_grad: float32 [1280, 2560], P('tile')
- fc2_grad: float32 [2560, 1280], P('tile')
Inputs may be any that keep to these rules, and one draw needn't show every extreme that they name: In each scene (all 8 chips of one index of the first dimension) exactly 1024 patches are visible; each chip has at most 256 visible patches, and in every scene one chip has exactly 256. Each chip's position ids are a permutation of its 512 positions.
All inputs are finite; a program needn't handle non-finite values.
Results may differ from a plain program's by a relative error of at most 0.007.
Values may be sent and summed in bfloat16 or wider, within the bound.
A program may use at most 128 MiB of HBM per device.

v0:
```python
import jax
import jax.numpy as jnp
from jax import lax
from jax.sharding import PartitionSpec as P

epsilon = 1e-06


def layer_norm(values, norm_gain, norm_bias):
    row_mean = jnp.mean(values, axis=-1, keepdims=True)
    centred = values - row_mean
    variance = jnp.mean(centred * centred, axis=-1, keepdims=True)
    inv_std = lax.rsqrt(variance + epsilon)
    scaled = centred * inv_std
    return (scaled * norm_gain + norm_bias, scaled, inv_std)


def norm_back(upstream, scaled, inv_std):
    mean_up = jnp.mean(upstream, axis=-1, keepdims=True)
    mean_cross = jnp.mean(upstream * scaled, axis=-1, keepdims=True)
    return inv_std * (upstream - mean_up - scaled * mean_cross)


def gelu_parts(pre_act):
    normal_cdf = 0.5 * (1.0 + lax.erf(pre_act * 0.7071067811865476))
    density = jnp.exp(-0.5 * pre_act * pre_act) * 0.3989422804014327
    return (pre_act * normal_cdf, normal_cdf + pre_act * density)


def encode(enc_input, enc_params):
    (
        mlp_gain,
        mlp_bias,
        fc1_weight,
        fc1_bias,
        fc2_weight,
        fc2_bias,
        encoder_gain,
        encoder_bias,
        embed_weight,
        embed_bias,
    ) = enc_params
    rows_in = enc_input.astype(jnp.float32)
    mlp_in, mlp_scaled, mlp_inv = layer_norm(rows_in, mlp_gain, mlp_bias)
    mlp_in = mlp_in.astype(jnp.bfloat16)
    pre_act = jnp.dot(mlp_in, fc1_weight, preferred_element_type=jnp.float32) + fc1_bias
    activation, slope = gelu_parts(pre_act)
    hidden = activation.astype(jnp.bfloat16)
    encoded = rows_in + jnp.dot(hidden, fc2_weight, preferred_element_type=jnp.float32) + fc2_bias
    normed, enc_scaled, enc_inv = layer_norm(encoded, encoder_gain, encoder_bias)
    normed = normed.astype(jnp.bfloat16)
    projected = (
        jnp.dot(normed, embed_weight, preferred_element_type=jnp.float32) + embed_bias
    ).astype(jnp.bfloat16)
    saved = (mlp_in, mlp_scaled, mlp_inv, slope, hidden, enc_scaled, enc_inv)
    return (saved, projected)


def encode_back(saved, grad_compact, enc_params):
    (
        mlp_gain,
        mlp_bias,
        fc1_weight,
        fc1_bias,
        fc2_weight,
        fc2_bias,
        encoder_gain,
        encoder_bias,
        embed_weight,
        embed_bias,
    ) = enc_params
    mlp_in, mlp_scaled, mlp_inv, slope, hidden, enc_scaled, enc_inv = saved
    grad_normed = jnp.dot(grad_compact, embed_weight.T, preferred_element_type=jnp.float32)
    grad_encoded = norm_back(grad_normed * encoder_gain, enc_scaled, enc_inv).astype(jnp.bfloat16)
    grad_hidden = jnp.dot(grad_encoded, fc2_weight.T, preferred_element_type=jnp.float32)
    grad_pre = (grad_hidden * slope).astype(jnp.bfloat16)
    grad_mlp_in = jnp.dot(grad_pre, fc1_weight.T, preferred_element_type=jnp.float32)
    grad_feats = (
        grad_encoded.astype(jnp.float32) + norm_back(grad_mlp_in * mlp_gain, mlp_scaled, mlp_inv)
    ).astype(jnp.bfloat16)
    fc1_term = jnp.dot(mlp_in.T, grad_pre, preferred_element_type=jnp.float32)
    fc2_term = jnp.dot(hidden.T, grad_encoded, preferred_element_type=jnp.float32)
    return (fc1_term, fc2_term, grad_feats)


def decoder_pass(
    projected_rows,
    keep_rows,
    position_ids,
    upstream,
    position_table,
    mask_token,
    decoder_gain,
    decoder_bias,
):
    table_ids = jnp.arange(position_table.shape[0], dtype=jnp.int32)[None, :]
    pick = (position_ids[:, None] == table_ids).astype(jnp.bfloat16)
    placed = jnp.dot(pick, position_table, preferred_element_type=jnp.float32)
    dec_input = jnp.where(keep_rows, projected_rows, mask_token) + placed
    decoded, dec_scaled, dec_inv = layer_norm(dec_input, decoder_gain, decoder_bias)
    grad_input = norm_back(upstream.astype(jnp.float32) * decoder_gain, dec_scaled, dec_inv)
    grad_projected = jnp.where(keep_rows, grad_input, 0.0).astype(jnp.bfloat16)
    return (decoded.astype(jnp.bfloat16), grad_projected)


def shards(
    features,
    visible,
    positions,
    cotangent,
    mlp_gain,
    mlp_bias,
    fc1_weight,
    fc1_bias,
    fc2_weight,
    fc2_bias,
    encoder_gain,
    encoder_bias,
    embed_weight,
    embed_bias,
    mask_token,
    position_table,
    decoder_gain,
    decoder_bias,
):
    patch_count = features.shape[2]
    model_width = features.shape[3]
    dec_width = embed_weight.shape[1]
    most_rows = patch_count // 2
    flags = visible.reshape(patch_count)
    row_data = features.reshape(patch_count, model_width)
    keep_rows = (flags > 0)[:, None]
    upstream = cotangent.reshape(patch_count, dec_width)
    ids = jnp.arange(patch_count, dtype=jnp.int32)
    row_rank = jnp.sum(jnp.where(ids[None, :] < ids[:, None], flags[None, :], 0), axis=1)
    slots = jnp.arange(most_rows, dtype=jnp.int32)
    target = jnp.where(flags > 0, row_rank, -1)
    gather = (slots[:, None] == target[None, :]).astype(jnp.bfloat16)
    scatter = (target[:, None] == slots[None, :]).astype(jnp.bfloat16)
    enc_params = (
        mlp_gain,
        mlp_bias,
        fc1_weight,
        fc1_bias,
        fc2_weight,
        fc2_bias,
        encoder_gain,
        encoder_bias,
        embed_weight,
        embed_bias,
    )
    decoder_args = (position_table, mask_token, decoder_gain, decoder_bias)
    enc_input = jnp.dot(gather, row_data, preferred_element_type=jnp.bfloat16)
    saved, projected = encode(enc_input, enc_params)
    projected_rows = jnp.dot(scatter, projected, preferred_element_type=jnp.float32)
    decoded, grad_projected = decoder_pass(
        projected_rows, keep_rows, positions.reshape(-1), upstream, *decoder_args
    )
    grad_compact = jnp.dot(gather, grad_projected, preferred_element_type=jnp.bfloat16)
    fc1_term, fc2_term, grad_feats = encode_back(saved, grad_compact, enc_params)
    grad_rows = jnp.dot(scatter, grad_feats, preferred_element_type=jnp.bfloat16)
    device_total = lax.axis_size("dp") * lax.axis_size("tile")
    totals = []
    for term in (fc1_term, fc2_term):
        share = lax.psum_scatter(term.astype(jnp.bfloat16), "tile", scatter_dimension=0, tiled=True)
        totals.append(lax.psum(share, "dp").astype(jnp.float32) / device_total)
    fc1_grad, fc2_grad = totals
    feature_grad = grad_rows.reshape(features.shape)
    decoded_out = decoded.reshape(cotangent.shape)
    return (feature_grad, decoded_out, fc1_grad, fc2_grad)


def solution(mesh):
    return jax.shard_map(
        shards,
        mesh=mesh,
        in_specs=(
            P("dp", "tile", None, None),
            P("dp", "tile", None),
            P("dp", "tile", None),
            P("dp", "tile", None, None),
            P(),
            P(),
            P(),
            P(),
            P(),
            P(),
            P(),
            P(),
            P(),
            P(),
            P(),
            P(),
            P(),
            P(),
        ),
        out_specs=(
            P("dp", "tile", None, None),
            P("dp", "tile", None, None),
            P("tile", None),
            P("tile", None),
        ),
        check_vma=False,
    )
```

profile of v0, /device:TPU:0, one launch (start us, length us, event | category | flops | bytes accessed | tf_op | source)
XLA Modules:
  0.0 269.7 jit_solution(12920631367889845395)
XLA Ops:
  7.2 0.0 copy-start
  7.2 0.0 reduce-scatter.3.cloned.1.call-start
  7.2 0.9 select_reduce_fusion
  8.1 0.7 broadcast_select_fusion
  8.8 1.9 fusion.60
  10.8 0.0 copy-start.9
  10.8 0.0 slice-start
  10.8 0.3 multiply_reduce_fusion.3
  11.1 0.4 copy-done.8
  11.4 0.0 copy-done.9
  11.5 0.0 copy-done.13
  11.5 5.2 %convolution_add_fusion = f32[256,2560]{1,0:T(8,128)S(1)} fusion(bf16[1280,2560]{1,0:T(8,128)(2,1)} %param.24, f32[2560]{0:T(1024)S(1)} %copy-done.13, f32[256,1280]{1,0:T(8,128)S(1)} %get-tuple-element.24, f32[1280]{0:T(1024)S(1)} %copy-done.8, f32[1280]{0:T(1024)S(1)} %copy-done.9, f32[256]{0:T(256)S(1)} %add_rsqrt_fusion.2, ...), kind=kOutput, calls=%fused_computation.3 | convolution fusion | flops 1680015360 | bytes 10508288 | tf_op jit(solution)/shard_map/dot_general | solution.py:46
  16.7 2.2 fusion.61
  18.9 0.0 copy-start.15
  18.9 0.0 copy-start.16
  19.0 1.0 copy-done.4
  20.0 0.3 multiply_reduce_fusion.2
  20.3 0.0 copy-start.7
  20.3 0.0 copy-start.10
  20.3 3.2 %convolution_select_fusion = f32[512,512]{0,1:T(8,128)} fusion(bf16[1280,512]{1,0:T(8,128)(2,1)S(1)} %copy-done, f32[256,1280]{1,0:T(8,128)} %copy-done.4, f32[1280]{0:T(1024)S(1)} %copy-done.15, f32[1280]{0:T(1024)S(1)} %copy-done.16, f32[256]{0:T(256)S(1)} %add_rsqrt_fusion.1, f32[256]{0:T(256)S(1)} %broadcast_multiply_fusion.7, f32[512]{0:T(512)S(1)} %copy-done.17, ...), kind=kOutput, calls=%fused_computation.21 | convolution fusion | flops 472055808 | bytes 3688960 | tf_op jit(solution)/shard_map/dot_general | solution.py:155
  23.6 1.9 fusion.62
  25.5 0.0 copy-start.1
  25.5 0.0 copy-start.11
  25.5 0.9 copy-done.1
  26.4 0.2 multiply_reduce_fusion.4
  26.6 1.3 copy.24
  27.9 2.4 fusion.12
  30.3 3.7 %fusion.59 = (f32[256]{0:T(256)S(1)}, f32[256]{0:T(256)S(1)}, f32[256,1280]{1,0:T(8,128)}) fusion(f32[256]{0:T(256)S(1)} %add_rsqrt_fusion.1, f32[256,1280]{1,0:T(8,128)} %copy-done.4, f32[256]{0:T(256)S(1)} %broadcast_multiply_fusion.7, f32[1280]{0:T(1024)S(1)} %copy-done.16, bf16[1280,512]{1,0:T(8,128)(2,1)S(1)} %copy-done, f32[512,512]{0,1:T(8,128)} %copy-done.1, ...), kind=kOutput, calls=%fused_computation.92 | convolution fusion | flops 474480128 | bytes 5527040 | tf_op jit(solution)/shard_map/dot_general | solution.py:73
  34.1 2.2 multiply_convert_fusion.1
  36.3 0.3 copy-done.3
  36.6 5.0 %fusion = bf16[256,2560]{1,0:T(8,128)(2,1)S(1)} fusion(bf16[256,1280]{1,0:T(8,128)(2,1)S(1)} %multiply_convert_fusion.1, bf16[2560,1280]{1,0:T(8,128)(2,1)} %param.26, f32[256,2560]{1,0:T(8,128)S(1)} %copy-done.3), kind=kOutput, calls=%fused_computation.5 | convolution fusion | flops 1684275200 | bytes 11141120 | tf_op jit(solution)/shard_map/dot_general | solution.py:75
  41.6 0.0 copy-start.5
  41.7 1.0 copy-done.5
  42.7 4.8 %convolution_convert_fusion.1 = bf16[1280,2560]{1,0:T(8,128)(2,1)} fusion(bf16[256,2560]{1,0:T(8,128)(2,1)S(1)} %fusion, f32[256,1280]{1,0:T(8,128)S(1)} %get-tuple-element.24, f32[1280]{0:T(1024)S(1)} %copy-done.8, f32[1280]{0:T(1024)S(1)} %copy-done.9, f32[256]{0:T(256)S(1)} %add_rsqrt_fusion.2, f32[256]{0:T(256)S(1)} %broadcast_multiply_fusion.8), kind=kOutput, calls=%fused_computation.1 | convolution fusion | flops 1682636800 | bytes 9187328 | tf_op jit(solution)/shard_map/dot_general | solution.py:81
  47.5 0.0 reduce-scatter.3.cloned.1.call-update
  47.5 0.2 reduce-scatter.5.cloned.1.call-start
  47.7 6.7 %convolution_convert_fusion = bf16[2560,1280]{1,0:T(8,128)(2,1)} fusion(bf16[256,1280]{1,0:T(8,128)(2,1)S(1)} %multiply_convert_fusion.1, f32[256,2560]{1,0:T(8,128)} %copy-done.2), kind=kOutput, calls=%fused_computation | convolution fusion | flops 1684275200 | bytes 9830400 | tf_op jit(solution)/shard_map/dot_general | solution.py:82
  54.4 0.0 reduce-scatter.5.cloned.1.call-update
  54.5 0.0 all-reduce.3.cloned.1.call-start
  54.5 68.1 %reduce-scatter.3.cloned.1.call-done = bf16[160,2560]{1,0:T(8,128)(2,1)} async-done(((bf16[1280,2560]{1,0:T(8,128)(2,1)}), bf16[160,2560]{1,0:T(8,128)(2,1)}) %reduce-scatter.3.cloned.1.call-update) | async-done | bytes 819216 | tf_op jit(solution)/shard_map/reduce_scatter | solution.py:165
  122.6 73.0 %reduce-scatter.5.cloned.1.call-done = bf16[320,1280]{1,0:T(8,128)(2,1)} async-done(((bf16[2560,1280]{1,0:T(8,128)(2,1)}), bf16[320,1280]{1,0:T(8,128)(2,1)}) %reduce-scatter.5.cloned.1.call-update) | async-done | bytes 819216 | tf_op jit(solution)/shard_map/reduce_scatter | solution.py:165
  195.6 0.0 all-reduce.3.cloned.1.call-update
  195.6 2.0 copy.25
  197.7 5.3 %fusion.58 = (f32[256]{0:T(256)S(1)}, f32[256]{0:T(256)S(1)}, f32[256,1280]{1,0:T(8,128)S(1)}) fusion(f32[256]{0:T(256)S(1)} %add_rsqrt_fusion.2, f32[256,1280]{1,0:T(8,128)S(1)} %get-tuple-element.24, f32[256]{0:T(256)S(1)} %broadcast_multiply_fusion.8, f32[1280]{0:T(1024)S(1)} %copy-done.9, bf16[256,2560]{1,0:T(8,128)(2,1)} %copy-done.5, ...), kind=kOutput, calls=%fused_computation.91 | convolution fusion | flops 1679687168 | bytes 10494976 | tf_op jit(solution)/shard_map/dot_general | solution.py:77
  203.0 2.0 convolution_bitcast_fusion
  205.0 54.3 %all-reduce.3.cloned.1.call-done = (bf16[160,2560]{1,0:T(8,128)(2,1)}, bf16[320,1280]{1,0:T(8,128)(2,1)}) async-done(((bf16[160,2560]{1,0:T(8,128)(2,1)}, bf16[320,1280]{1,0:T(8,128)(2,1)}), (bf16[160,2560]{1,0:T(8,128)(2,1)}, bf16[320,1280]{1,0:T(8,128)(2,1)})) %all-reduce.3.cloned.1.call-update) | async-done | bytes 1638416 | tf_op jit(solution)/shard_map/psum | solution.py:166
  259.3 2.5 convert_multiply_fusion
  261.8 1.3 convert_multiply_fusion.1
  (37 shorter events, 0.1 us)
Async XLA Ops:
  7.2 13.1 %copy-start = (bf16[1280,512]{1,0:T(8,128)(2,1)S(1)}, bf16[1280,512]{1,0:T(8,128)(2,1)}, u32[]{:S(2)}) copy-start(bf16[1280,512]{1,0:T(8,128)(2,1)} %param.30) | copy-start | bytes 3932164
  7.2 115.5 %reduce-scatter.3.cloned.1.call-start = ((), (), s32[]{:S(2)}) async-start(), calls=%async_computation.2 | async-start | bytes 7372800 | tf_op jit(solution)/shard_map/reduce_scatter | solution.py:165
  10.7 0.7 copy-start.8
  10.8 0.7 copy-start.9
  10.8 0.7 copy-start.13
  10.8 5.9 %slice-start = ((s8[6553600]{0:T(1024)(128)(4,1)}), s8[4194304]{0:T(1024)(128)(4,1)S(1)}, s32[]{:S(2)}) async-start(s8[6553600]{0:T(1024)(128)(4,1)} %bitcast.36), calls=%async_computation.5 | async-start | bytes 8388608
  11.5 5.2 %slice-start.1 = ((s8[6553600]{0:T(1024)(128)(4,1)}), s8[2359296]{0:T(1024)(128)(4,1)S(1)}, s32[]{:S(2)}) async-start(s8[6553600]{0:T(1024)(128)(4,1)} %bitcast.36), calls=%async_computation.6 | async-start | bytes 4718592
  11.5 5.2 %copy-start.14 = (f32[1280]{0:T(1024)S(1)}, f32[1280]{0:T(1024)}, u32[]{:S(2)}) copy-start(f32[1280]{0:T(1024)} %param.27) | copy-start | bytes 15364
  16.7 2.2 copy-start.2
  18.9 1.1 copy-start.4
  18.9 1.3 copy-start.15
  18.9 1.3 copy-start.16
  19.0 1.3 copy-start.17
  19.0 1.3 copy-start.18
  20.3 3.3 %copy-start.7 = (bf16[512,512]{1,0:T(8,128)(2,1)S(1)}, bf16[512,512]{1,0:T(8,128)(2,1)}, u32[]{:S(2)}) copy-start(bf16[512,512]{1,0:T(8,128)(2,1)} %param.33) | copy-start | bytes 1572868
  20.3 3.2 %copy-start.10 = (s32[1,1,512]{2,1,0:T(1,128)S(1)}, s32[1,1,512]{2,1,0:T(1,128)}, u32[]{:S(2)}) copy-start(s32[1,1,512]{2,1,0:T(1,128)} %param.20) | copy-start | bytes 6148
  25.5 1.0 copy-start.1
  25.5 2.4 copy-start.11
  25.5 2.4 copy-start.12
  34.1 2.5 copy-start.3
  41.6 1.1 copy-start.5
  47.5 148.1 %reduce-scatter.5.cloned.1.call-start = ((), (), s32[]{:S(2)}) async-start(), calls=%async_computation.3 | async-start | bytes 7372800 | tf_op jit(solution)/shard_map/reduce_scatter | solution.py:165
  54.5 204.9 %all-reduce.3.cloned.1.call-start = ((), (), s32[]{:S(2)}) async-start(), calls=%async_computation.4 | async-start | bytes 3276800 | tf_op jit(solution)/shard_map/psum | solution.py:166
  259.3 2.5 copy-start.6
Sparse Core Ops, SparseCore 0:
  47.6 74.9 reduce-scatter.2
  125.0 70.6 reduce-scatter.4
  198.8 60.5 all-reduce.2
where the time goes:
time: 270 us
  waiting for transfers between devices  195 us (72%)
  matrix products  41.9 us (16%)
  between operations  14.1 us (5%)
  other arithmetic  10.9 us (4%)
  local copies, waits for them, and re-layouts  7.04 us (3%)
    reduce_scatter x2, waiting for transfers between devices, shards(): lax.psum_scatter(term.astype(jnp.bfloat16), 'tile', scatter_dimension=0,...  141 us
    psum x1, waiting for transfers between devices, shards(): totals.append(lax.psum(share, 'dp').astype(jnp.float32) / device_total)  54.3 us
    unnamed x44, local copies, waits for them, and re-layouts  7.04 us
    dot_general x1, matrix products, encode_back(): jnp.dot(hidden.T, grad_encoded, preferred_element_type=jnp.float32)  6.71 us
  transfers between devices with their start and end apart: 3, of which 3 were waited for; matrix products, arithmetic and copies ran while one was open for 6% of the time, Pallas kernels for 0%

commit v1 on v0

--- a/solution.py
+++ b/solution.py
@@ -163,7 +163,9 @@
     totals = []
     for term in (fc1_term, fc2_term):
         share = lax.psum_scatter(term.astype(jnp.bfloat16), "tile", scatter_dimension=0, tiled=True)
-        totals.append(lax.psum(share, "dp").astype(jnp.float32) / device_total)
+        totals.append(
+            jnp.sum(lax.all_gather(share, "dp"), axis=0).astype(jnp.float32) / device_total
+        )
     fc1_grad, fc2_grad = totals
     feature_grad = grad_rows.reshape(features.shape)
     decoded_out = decoded.reshape(cotangent.shape)

time: 270 us -> 290 us (1.074)
  waiting for transfers between devices: 195 us -> 213 us
    all_gather x0 -> x2, waiting for transfers between devices: none -> 78.6 us  [shards(): lax.all_gather(share, 'dp')]
    psum x1 -> x0, waiting for transfers between devices: 54.3 us -> none  [shards(): totals.append(lax.psum(share, 'dp').astype(jnp.float32) / device_total)]
    reduce_scatter x2, waiting for transfers between devices: 141 us -> 134 us  [shards(): lax.psum_scatter(term.astype(jnp.bfloat16), 'tile', scatter_dimension=0,...]
    reduce_sum x0 -> x2, other arithmetic: none -> 5.3 us  [shards(): jnp.sum(lax.all_gather(share, 'dp'), axis=0).astype(jnp.float32)]
    unnamed x44 -> x40, local copies, waits for them, and re-layouts: 7.04 us -> 6.1 us
  transfers between devices with their start and end apart: 3 -> 4, of which waited for: 3 -> 4; matrix products, arithmetic and copies ran while one was open for 6% -> 9% of each run, Pallas kernels for 0% -> 0%
where the time goes in v1:
time: 290 us; the launch traced here: 289 us
  waiting for transfers between devices  213 us (73%)
  matrix products  42.2 us (15%)
  between operations  14.1 us (5%)
  other arithmetic  13.7 us (5%)
  local copies, waits for them, and re-layouts  6.1 us (2%)
    reduce_scatter x2, waiting for transfers between devices, shards(): lax.psum_scatter(term.astype(jnp.bfloat16), 'tile', scatter_dimension=0,...  134 us
    all_gather x2, waiting for transfers between devices, shards(): lax.all_gather(share, 'dp')  78.6 us
    dot_general x1, matrix products, encode_back(): jnp.dot(grad_encoded, fc2_weight.T, preferred_element_type=jnp.float32)  7.8 us
    unnamed x40, local copies, waits for them, and re-layouts  6.1 us
  transfers between devices with their start and end apart: 4, of which 4 were waited for; matrix products, arithmetic and copies ran while one was open for 9% of the time, Pallas kernels for 0%

profile of v1, /device:TPU:0, one launch (start us, length us, event | category | flops | bytes accessed | tf_op | source)
XLA Modules:
  0.0 289.2 jit_solution(1139976037994404412)
XLA Ops:
  7.2 0.0 copy-start
  7.2 0.0 reduce-scatter.5.cloned.1.call-start
  7.2 0.9 select_reduce_fusion
  8.1 0.7 broadcast_select_fusion
  8.8 1.3 copy.24
  10.1 1.9 fusion.60
  12.0 0.0 copy-start.7
  12.1 0.0 slice-start
  12.1 0.3 multiply_reduce_fusion.3
  12.4 0.4 copy-done.6
  12.7 0.0 copy-done.7
  12.7 0.0 copy-done.11
  12.8 5.2 %convolution_add_fusion = f32[256,2560]{1,0:T(8,128)S(1)} fusion(bf16[1280,2560]{1,0:T(8,128)(2,1)} %param.24, f32[2560]{0:T(1024)S(1)} %copy-done.11, f32[256,1280]{1,0:T(8,128)S(1)} %get-tuple-element.22, f32[1280]{0:T(1024)S(1)} %copy-done.6, f32[1280]{0:T(1024)S(1)} %copy-done.7, f32[256]{0:T(256)S(1)} %add_rsqrt_fusion.2, ...), kind=kOutput, calls=%fused_computation.3 | convolution fusion | flops 1680015360 | bytes 10508288 | tf_op jit(solution)/shard_map/dot_general | solution.py:46
  18.0 2.1 fusion.61
  20.2 0.0 copy-start.14
  20.2 0.0 copy-start.15
  20.2 1.0 copy-done.4
  21.2 0.3 multiply_reduce_fusion.2
  21.5 3.2 %convolution_select_fusion = f32[512,512]{0,1:T(8,128)} fusion(bf16[1280,512]{1,0:T(8,128)(2,1)S(1)} %copy-done, f32[256,1280]{1,0:T(8,128)} %copy-done.4, f32[1280]{0:T(1024)S(1)} %copy-done.13, f32[1280]{0:T(1024)S(1)} %copy-done.14, f32[256]{0:T(256)S(1)} %add_rsqrt_fusion.1, f32[256]{0:T(256)S(1)} %broadcast_multiply_fusion.7, f32[512]{0:T(512)S(1)} %copy-done.15, ...), kind=kOutput, calls=%fused_computation.21 | convolution fusion | flops 472055808 | bytes 3688960 | tf_op jit(solution)/shard_map/dot_general | solution.py:155
  24.7 2.1 fusion.62
  26.8 0.2 multiply_reduce_fusion.4
  27.0 1.2 fusion.12
  28.2 3.7 %fusion.59 = (f32[256]{0:T(256)S(1)}, f32[256]{0:T(256)S(1)}, f32[256,1280]{1,0:T(8,128)}) fusion(f32[256]{0:T(256)S(1)} %add_rsqrt_fusion.1, f32[256,1280]{1,0:T(8,128)} %copy-done.4, f32[256]{0:T(256)S(1)} %broadcast_multiply_fusion.7, f32[1280]{0:T(1024)S(1)} %copy-done.14, bf16[1280,512]{1,0:T(8,128)(2,1)S(1)} %copy-done, f32[512,512]{0,1:T(8,128)} %copy-done.1, ...), kind=kOutput, calls=%fused_computation.92 | convolution fusion | flops 474480128 | bytes 5527040 | tf_op jit(solution)/shard_map/dot_general | solution.py:73
  32.0 2.2 multiply_convert_fusion.1
  34.2 0.3 copy-done.3
  34.5 4.2 %convolution_convert_fusion = bf16[2560,1280]{1,0:T(8,128)(2,1)} fusion(bf16[256,1280]{1,0:T(8,128)(2,1)S(1)} %multiply_convert_fusion.1, f32[256,2560]{1,0:T(8,128)S(1)} %copy-done.3), kind=kOutput, calls=%fused_computation | convolution fusion | flops 1684275200 | bytes 9830400 | tf_op jit(solution)/shard_map/dot_general | solution.py:82
  38.7 0.0 reduce-scatter.5.cloned.1.call-update
  38.7 0.2 reduce-scatter.3.cloned.1.call-start
  38.9 7.8 %fusion = bf16[256,2560]{1,0:T(8,128)(2,1)S(1)} fusion(bf16[256,1280]{1,0:T(8,128)(2,1)S(1)} %multiply_convert_fusion.1, bf16[2560,1280]{1,0:T(8,128)(2,1)} %param.26, f32[256,2560]{1,0:T(8,128)} %copy-done.2), kind=kOutput, calls=%fused_computation.5 | convolution fusion | flops 1684275200 | bytes 11141120 | tf_op jit(solution)/shard_map/dot_general | solution.py:75
  46.7 0.0 copy-start.5
  46.7 1.0 copy-done.5
  47.8 4.7 %convolution_convert_fusion.1 = bf16[1280,2560]{1,0:T(8,128)(2,1)} fusion(bf16[256,2560]{1,0:T(8,128)(2,1)S(1)} %fusion, f32[256,1280]{1,0:T(8,128)S(1)} %get-tuple-element.22, f32[1280]{0:T(1024)S(1)} %copy-done.6, f32[1280]{0:T(1024)S(1)} %copy-done.7, f32[256]{0:T(256)S(1)} %add_rsqrt_fusion.2, f32[256]{0:T(256)S(1)} %broadcast_multiply_fusion.8), kind=kOutput, calls=%fused_computation.1 | convolution fusion | flops 1682636800 | bytes 9187328 | tf_op jit(solution)/shard_map/dot_general | solution.py:81
  52.5 0.0 reduce-scatter.3.cloned.1.call-update
  52.6 0.0 all-gather.7.cloned.1.call-start
  52.6 61.2 %reduce-scatter.5.cloned.1.call-done = bf16[320,1280]{1,0:T(8,128)(2,1)} async-done(((bf16[2560,1280]{1,0:T(8,128)(2,1)}), bf16[320,1280]{1,0:T(8,128)(2,1)}) %reduce-scatter.5.cloned.1.call-update) | async-done | bytes 819216 | tf_op jit(solution)/shard_map/reduce_scatter | solution.py:165
  113.8 0.0 all-gather.7.cloned.1.call-update
  113.8 0.0 all-gather.5.cloned.1.call-start
  113.9 72.9 %reduce-scatter.3.cloned.1.call-done = bf16[160,2560]{1,0:T(8,128)(2,1)} async-done(((bf16[1280,2560]{1,0:T(8,128)(2,1)}), bf16[160,2560]{1,0:T(8,128)(2,1)}) %reduce-scatter.3.cloned.1.call-update) | async-done | bytes 819216 | tf_op jit(solution)/shard_map/reduce_scatter | solution.py:165
  186.8 0.0 all-gather.5.cloned.1.call-update
  186.8 2.0 copy.25
  188.9 5.3 %fusion.58 = (f32[256]{0:T(256)S(1)}, f32[256]{0:T(256)S(1)}, f32[256,1280]{1,0:T(8,128)S(1)}) fusion(f32[256]{0:T(256)S(1)} %add_rsqrt_fusion.2, f32[256,1280]{1,0:T(8,128)S(1)} %get-tuple-element.22, f32[256]{0:T(256)S(1)} %broadcast_multiply_fusion.8, f32[1280]{0:T(1024)S(1)} %copy-done.7, bf16[256,2560]{1,0:T(8,128)(2,1)} %copy-done.5, ...), kind=kOutput, calls=%fused_computation.91 | convolution fusion | flops 1679687168 | bytes 10494976 | tf_op jit(solution)/shard_map/dot_general | solution.py:77
  194.2 2.0 convolution_bitcast_fusion
  196.1 36.0 %all-gather.7.cloned.1.call-done = bf16[1280,1280]{1,0:T(8,128)(2,1)} async-done(((bf16[320,1280]{1,0:T(8,128)(2,1)}), bf16[1280,1280]{1,0:T(8,128)(2,1)}) %all-gather.7.cloned.1.call-update) | async-done | bytes 3276816 | tf_op jit(solution)/shard_map/all_gather | solution.py:167
  232.1 2.8 reduce_sum.155
  234.9 1.3 convert_multiply_fusion
  236.2 42.7 %all-gather.5.cloned.1.call-done = bf16[640,2560]{1,0:T(8,128)(2,1)} async-done(((bf16[160,2560]{1,0:T(8,128)(2,1)}), bf16[640,2560]{1,0:T(8,128)(2,1)}) %all-gather.5.cloned.1.call-update) | async-done | bytes 3276816 | tf_op jit(solution)/shard_map/all_gather | solution.py:167
  278.9 2.5 reduce_sum.154
  281.4 1.3 convert_multiply_fusion.1
  (38 shorter events, 0.1 us)
Async XLA Ops:
  7.2 14.3 %copy-start = (bf16[1280,512]{1,0:T(8,128)(2,1)S(1)}, bf16[1280,512]{1,0:T(8,128)(2,1)}, u32[]{:S(2)}) copy-start(bf16[1280,512]{1,0:T(8,128)(2,1)} %param.30) | copy-start | bytes 3932164
  7.2 106.6 %reduce-scatter.5.cloned.1.call-start = ((), (), s32[]{:S(2)}) async-start(), calls=%async_computation.3 | async-start | bytes 7372800 | tf_op jit(solution)/shard_map/reduce_scatter | solution.py:165
  12.0 0.7 copy-start.6
  12.0 0.7 copy-start.7
  12.0 0.7 copy-start.11
  12.1 5.9 %slice-start = ((s8[6553600]{0:T(1024)(128)(4,1)}), s8[4194304]{0:T(1024)(128)(4,1)S(1)}, s32[]{:S(2)}) async-start(s8[6553600]{0:T(1024)(128)(4,1)} %bitcast.40), calls=%async_computation.6 | async-start | bytes 8388608
  12.8 5.2 %slice-start.1 = ((s8[6553600]{0:T(1024)(128)(4,1)}), s8[2359296]{0:T(1024)(128)(4,1)S(1)}, s32[]{:S(2)}) async-start(s8[6553600]{0:T(1024)(128)(4,1)} %bitcast.40), calls=%async_computation.7 | async-start | bytes 4718592
  12.8 5.2 %copy-start.12 = (f32[1280]{0:T(1024)S(1)}, f32[1280]{0:T(1024)}, u32[]{:S(2)}) copy-start(f32[1280]{0:T(1024)} %param.27) | copy-start | bytes 15364
  18.0 2.2 copy-start.2
  20.1 1.1 copy-start.4
  20.2 1.3 copy-start.13
  20.2 1.3 copy-start.14
  20.2 1.3 copy-start.15
  20.2 1.3 copy-start.16
  21.5 3.2 %copy-start.8 = (s32[1,1,512]{2,1,0:T(1,128)S(1)}, s32[1,1,512]{2,1,0:T(1,128)}, u32[]{:S(2)}) copy-start(s32[1,1,512]{2,1,0:T(1,128)} %param.20) | copy-start | bytes 6148
  24.7 2.3 copy-start.9
  24.7 2.3 copy-start.10
  26.8 1.4 copy-start.1
  32.0 2.5 copy-start.3
  38.7 148.1 %reduce-scatter.3.cloned.1.call-start = ((), (), s32[]{:S(2)}) async-start(), calls=%async_computation.2 | async-start | bytes 7372800 | tf_op jit(solution)/shard_map/reduce_scatter | solution.py:165
  46.7 1.1 copy-start.5
  52.6 179.5 %all-gather.7.cloned.1.call-start = ((), (), s32[]{:S(2)}) async-start(), calls=%async_computation.5 | async-start | bytes 4096000 | tf_op jit(solution)/shard_map/all_gather | solution.py:167
  113.8 165.1 %all-gather.5.cloned.1.call-start = ((), (), s32[]{:S(2)}) async-start(), calls=%async_computation.4 | async-start | bytes 4096000 | tf_op jit(solution)/shard_map/all_gather | solution.py:167
Sparse Core Ops, SparseCore 0:
  38.8 74.9 reduce-scatter.4
  116.1 70.6 reduce-scatter.2
  188.6 43.4 all-gather.6
  233.8 45.0 all-gather.4
